TPU v7x, 512 devices: a whole 4x4x16 slice. The times are simulated.
512 devices in a mesh: dp: 64 (over z_lo, y, core), tile: 8 (over x, z_hi).
Axes of the slice: x: 4, y: 4, z: 16 (z_hi: 2, z_lo: 8; z = z_hi * 8 + z_lo), core: 2. Of those that a mesh axis runs over, the one named last changes fastest.
Arguments:
- frames: bfloat16 [64, 2, 3, 128, 128], P('dp', None, None, 'tile'), may hold values from 0 to 1
- features: bfloat16 [64, 64, 128, 128], P('dp', None, 'tile'), may hold values from -16 to 16
- cotangent: float32 [64, 3, 128, 128], P('dp', None, 'tile'), may hold values from -6 to 6
- head_weight: bfloat16 [108, 576], replicated, may hold values from -0.25 to 0.25
Outputs:
- grad_weight: float32 [108, 576], replicated
- grad_features: float32 [64, 64, 128, 128], P('dp', None, 'tile')
- grad_frames: float32 [64, 2, 3, 128, 128], P('dp', None, None, 'tile')
All inputs are finite; a program needn't handle non-finite values.
Results may differ from a plain program's by a relative error of at most 0.003.
Values may be sent and summed in bfloat16 or wider, within the bound.
No kernel may reach another device: no remote copies, remote signals or barrier semaphores. Data moves between devices by JAX's collectives and lax.ppermute only.
A program may use at most 64 MiB of HBM per device.

v0:
```python
import jax
import jax.numpy as jnp
from jax import lax
from jax.sharding import PartitionSpec as P


def with_halo(cells, sides, width):
    for axis, dim in sides:
        count = lax.axis_size(axis)
        ends = count - 1
        head = lax.slice_in_dim(cells, 0, width, axis=dim)
        tail = lax.slice_in_dim(cells, cells.shape[dim] - width, cells.shape[dim], axis=dim)
        cells = jnp.concatenate(
            [
                lax.ppermute(tail, axis, [(i, (i + 1) % count) for i in range(ends)]),
                cells,
                lax.ppermute(head, axis, [((i + 1) % count, i) for i in range(ends)]),
            ],
            axis=dim,
        )
    return cells


def from_behind(value, axis, steps):
    count = lax.axis_size(axis)
    leading, last = (max(0, -steps), min(count, count - steps))
    return lax.ppermute(value, axis, [(source, source + steps) for source in range(leading, last)])


def make_patches(padded_map, row_count, col_count):
    blocks = []
    for row_shift in range(3):
        for col_shift in range(3):
            piece = padded_map[
                :, row_shift : row_shift + row_count, col_shift : col_shift + col_count
            ]
            blocks.append(piece.reshape(piece.shape[0], row_count * col_count))
    return jnp.concatenate(blocks, 0)


def fold_patches(patch_grad, channels, row_count, col_count):
    folded = jnp.zeros((channels, row_count + 2, col_count + 2), jnp.float32)
    slot_index = 0
    for row_shift in range(3):
        for col_shift in range(3):
            block = patch_grad[slot_index * channels : (slot_index + 1) * channels].reshape(
                channels, row_count, col_count
            )
            folded = folded.at[
                :, row_shift : row_shift + row_count, col_shift : col_shift + col_count
            ].add(block)
            slot_index += 1
    return folded


def separable_grads(padded, vertical, horizontal, upstream, group_size):
    tap_count = vertical.shape[0]
    row_count = upstream.shape[1]
    col_count = upstream.shape[2]

    def one_tap(tap_index, carried):
        grad_vert, grad_horiz, grad_padded = carried
        tap_band = lax.dynamic_slice_in_dim(padded, tap_index, row_count, 1)
        scaled = lax.dynamic_index_in_dim(vertical, tap_index, 0, keepdims=False)[None] * upstream
        blended = jnp.zeros(upstream.shape, jnp.float32)
        back_sum = jnp.zeros((3, row_count, col_count + tap_count - 1), jnp.float32)
        horiz_rows = []
        for col_tap in range(tap_count):
            shifted = tap_band[:, :, col_tap : col_tap + col_count]
            weight_row = horizontal[col_tap][None]
            blended = blended + weight_row * shifted
            horiz_rows.append(jnp.sum(scaled * shifted, 0))
            back_sum = back_sum + jnp.pad(
                weight_row * scaled, ((0, 0), (0, 0), (col_tap, tap_count - 1 - col_tap))
            )
        grad_vert = lax.dynamic_update_slice_in_dim(
            grad_vert, jnp.sum(upstream * blended, 0)[None], tap_index, 0
        )
        grad_horiz = grad_horiz + jnp.stack(horiz_rows)
        old_rows = lax.dynamic_slice_in_dim(grad_padded, tap_index, row_count, 1)
        grad_padded = lax.dynamic_update_slice_in_dim(
            grad_padded, old_rows + back_sum, tap_index, 1
        )
        return (grad_vert, grad_horiz, grad_padded)

    def group_step(group_index, carried):
        for offset in range(group_size):
            carried = one_tap(group_index * group_size + offset, carried)
        return carried

    start_state = (
        jnp.zeros(vertical.shape, jnp.float32),
        jnp.zeros(vertical.shape, jnp.float32),
        jnp.zeros(padded.shape, jnp.float32),
    )
    return lax.fori_loop(0, tap_count // group_size, group_step, start_state)


def shards(frames, features, cotangent, head_weight):
    tap_count = head_weight.shape[0] // 4
    rim_rows = (tap_count - 1) // 2
    kernel_scale = tap_count ** (-0.5)
    feature_map = features[0]
    channels, row_count, col_count = feature_map.shape
    upstream = cotangent[0]
    feature_ext = with_halo(feature_map, (("tile", 1),), 1)
    frame_ext = with_halo(frames[0], (("tile", 2),), rim_rows)
    patches = make_patches(jnp.pad(feature_ext, ((0, 0), (0, 0), (1, 1))), row_count, col_count)
    kernels = jnp.dot(head_weight, patches, preferred_element_type=jnp.float32).reshape(
        -1, row_count, col_count
    )
    grad_list = []
    frame_list = []
    for which_frame in range(2):
        vertical = (
            kernels[2 * which_frame * tap_count : (2 * which_frame + 1) * tap_count] * kernel_scale
        )
        horizontal = (
            kernels[(2 * which_frame + 1) * tap_count : (2 * which_frame + 2) * tap_count]
            * kernel_scale
        )
        padded = jnp.pad(
            frame_ext[which_frame].astype(jnp.float32), ((0, 0), (0, 0), (rim_rows, rim_rows))
        )
        grad_vert, grad_horiz, grad_padded = separable_grads(
            padded, vertical, horizontal, upstream, 3
        )
        grad_list += [grad_vert, grad_horiz]
        frame_list.append(grad_padded[:, :, rim_rows : rim_rows + col_count])
    kernel_grad = (jnp.concatenate(grad_list, 0) * kernel_scale).astype(jnp.bfloat16)
    out_channels = kernel_grad.shape[0]
    flat_grad = kernel_grad.reshape(out_channels, row_count * col_count)
    weight_part = lax.dot_general(
        flat_grad, patches, (((1,), (1,)), ((), ())), preferred_element_type=jnp.float32
    )
    weight_sum = lax.psum(weight_part, ("dp", "tile"))
    pixel_count = lax.axis_size("dp") * lax.axis_size("tile") * row_count * col_count
    weight_sum = weight_sum * pixel_count ** (-0.5)
    image_grad = jnp.stack(frame_list)
    top_rim = image_grad[:, :, :rim_rows]
    bottom_rim = image_grad[:, :, rim_rows + row_count :]
    middle = image_grad[:, :, rim_rows : rim_rows + row_count]
    patch_grad = lax.dot_general(
        head_weight, flat_grad, (((0,), (0,)), ((), ())), preferred_element_type=jnp.float32
    )
    feature_pad = fold_patches(patch_grad, channels, row_count, col_count)[:, :, 1 : col_count + 1]
    from_above = from_behind((bottom_rim, feature_pad[:, row_count + 1 :]), "tile", 1)
    from_below = from_behind((top_rim, feature_pad[:, :1]), "tile", -1)
    feat_grad = feature_pad[:, 1 : row_count + 1]
    feat_grad = feat_grad.at[:, :1].add(from_above[1]).at[:, row_count - 1 :].add(from_below[1])
    above_image = from_above[0]
    below_image = from_below[0]
    middle = (
        middle.at[:, :, :rim_rows]
        .add(above_image)
        .at[:, :, row_count - rim_rows :]
        .add(below_image)
    )
    return (weight_sum, feat_grad[None], middle[None])


def solution(mesh):
    in_specs = (
        P("dp", None, None, "tile", None),
        P("dp", None, "tile", None),
        P("dp", None, "tile", None),
        P(),
    )
    out_specs = (P(), P("dp", None, "tile", None), P("dp", None, None, "tile", None))
    return jax.shard_map(shards, mesh=mesh, in_specs=in_specs, out_specs=out_specs, check_vma=False)
```

profile of v0, /device:TPU:1, one launch (start us, length us, event | category | flops | bytes accessed | tf_op | source)
XLA Modules:
  0.0 782.7 jit_solution(13102594171610701222)
XLA Ops:
  8.1 16.3 %collective-permute-start.2 = (bf16[2,3,13,128]{3,2,1,0:T(8,128)(2,1)S(1)}, bf16[2,3,13,128]{3,2,1,0:T(8,128)(2,1)S(1)}, u32[]{:S(2)}, u32[]{:S(2)}) collective-permute-start(bf16[2,3,13,128]{3,2,1,0:T(8,128)(2,1)S(1)} %get-tuple-element.1178), channel_id=1, source_target_pairs={{0,1},{1,2},{2,3},{3,4},{4,5},{5,6},{6,7},{8,9},{9,10},{10,11},{11... | collective-permute-start | bytes 59912 | tf_op jit(solution)/shard_map/ppermute | solution.py:15
  26.6 12.7 %collective-permute-start = (bf16[64,1,128]{2,1,0:T(2,128)(2,1)S(1)}, bf16[64,1,128]{2,1,0:T(2,128)(2,1)S(1)}, u32[]{:S(2)}, u32[]{:S(2)}) collective-permute-start(bf16[64,1,128]{2,1,0:T(2,128)(2,1)S(1)} %get-tuple-element.1172), channel_id=1, source_target_pairs={{0,1},{1,2},{2,3},{3,4},{4,5},{5,6},{6,7},{8,9},{9,10},{10,11},{11... | collective-permute-start | bytes 49160 | tf_op jit(solution)/shard_map/ppermute | solution.py:15
  43.4 9.4 %collective-permute-done.1 = bf16[64,1,128]{2,1,0:T(2,128)(2,1)S(1)} collective-permute-done((bf16[64,1,128]{2,1,0:T(2,128)(2,1)S(1)}, bf16[64,1,128]{2,1,0:T(2,128)(2,1)S(1)}, u32[]{:S(2)}, u32[]{:S(2)}) %collective-permute-start.1) | collective-permute-done | bytes 16416 | tf_op jit(solution)/shard_map/ppermute | solution.py:17
  52.7 1.6 fusion.16
  58.5 59.1 %while.54 = (s32[]{:T(128)}, f32[27,16,128]{2,1,0:T(8,128)S(1)}, f32[27,16,128]{2,1,0:T(8,128)S(1)}, f32[3,42,154]{2,1,0:T(8,128)S(1)}, f32[27,16,128]{2,1,0:T(8...) while((s32[]{:T(128)}, f32[27,16,128]{2,1,0:T(8,128)S(1)}, ...), condition=%wide.region_171.172_spmd.clone, body=%wide.region_86.171_spmd.clone.sunk | while | flops 3173135 | bytes 13660168 | solution.py:96
  120.0 129.0 %while.53 = (s32[]{:T(128)}, f32[27,16,128]{2,1,0:T(8,128)}, f32[27,16,128]{2,1,0:T(8,128)S(1)}, f32[3,42,154]{2,1,0:T(8,128)S(1)}, f32[27,16,128]{2,1,0:T(8,128...) while((s32[]{:T(128)}, f32[27,16,128]{2,1,0:T(8,128)}, ...), condition=%wide.region_85.86_spmd.clone, body=%wide.region_0.85_spmd.clone.sunk | while | flops 3173135 | bytes 13856832 | solution.py:96
  130.9 1.5 add_add_fusion.13
  145.2 1.5 add_add_fusion.13
  159.5 1.5 add_add_fusion.13
  173.8 1.5 add_add_fusion.13
  188.1 1.5 add_add_fusion.13
  202.4 1.5 add_add_fusion.13
  216.7 1.5 add_add_fusion.13
  231.0 1.5 add_add_fusion.13
  245.3 1.5 add_add_fusion.13
  251.0 2.7 fusion.26
  253.7 1.9 convolution_bitcast_fusion
  256.4 1.6 slice_bitcast_fusion.54
  258.2 2.4 bitcast_add_fusion.6
  260.6 6.1 scatter-add.45
  266.6 3.1 add_select_fusion
  269.8 5.1 scatter-add.46
  276.1 2.1 bitcast_add_fusion.4
  278.2 4.7 scatter-add.50
  283.9 4.7 scatter-add.51
  288.9 3.9 scatter-add.55
  293.0 3.9 scatter-add.56
  296.9 4.0 collective-permute-start.4
  301.2 11.2 %collective-permute-start.6 = (f32[2,3,13,128]{3,2,1,0:T(8,128)S(1)}, f32[2,3,13,128]{3,2,1,0:T(8,128)S(1)}, u32[]{:S(2)}, u32[]{:S(2)}) collective-permute-start(f32[2,3,13,128]{3,2,1,0:T(8,128)S(1)} %fusion.19), channel_id=1, source_target_pairs={{0,1},{1,2},{2,3},{3,4},{4,5},{5,6},{6,7},{8,9},{9,10},{10,11},{11... | collective-permute-start | bytes 119816 | tf_op jit(solution)/shard_map/ppermute | solution.py:27
  315.1 11.2 %collective-permute-done.5 = f32[64,1,128]{2,0,1:T(8,128)S(1)} collective-permute-done((f32[64,1,128]{2,0,1:T(8,128)S(1)}, f32[64,1,128]{2,0,1:T(8,128)S(1)}, u32[]{:S(2)}, u32[]{:S(2)}) %collective-permute-start.5) | collective-permute-done | bytes 32800 | tf_op jit(solution)/shard_map/ppermute | solution.py:27
  328.3 445.8 %all-reduce.168.cloned.1.call-done = f32[108,576]{1,0:T(8,128)} async-done(((f32[108,576]{1,0:T(8,128)}), f32[108,576]{1,0:T(8,128)}) %all-reduce.168.cloned.1.call-update) | async-done | bytes 248848 | tf_op jit(solution)/shard_map/psum | solution.py:136
  774.1 1.7 broadcast_multiply_fusion.168
  (2027 shorter events, 184.5 us)
Async XLA Ops:
  7.2 48.6 %copy-start = (bf16[108,576]{1,0:T(8,128)(2,1)S(1)}, bf16[108,576]{1,0:T(8,128)(2,1)}, u32[]{:S(2)}) copy-start(bf16[108,576]{1,0:T(8,128)(2,1)} %param.37) | copy-start | bytes 373252
  7.2 767.0 %all-reduce.168.cloned.1.call-start = ((), (), s32[]{:S(2)}) async-start(), calls=%async_computation | async-start | bytes 573440 | tf_op jit(solution)/shard_map/psum | solution.py:136
  8.1 50.2 %collective-permute-start.2 = (bf16[2,3,13,128]{3,2,1,0:T(8,128)(2,1)S(1)}, bf16[2,3,13,128]{3,2,1,0:T(8,128)(2,1)S(1)}, u32[]{:S(2)}, u32[]{:S(2)}) collective-permute-start(bf16[2,3,13,128]{3,2,1,0:T(8,128)(2,1)S(1)} %get-tuple-element.1178), channel_id=1, source_target_pairs={{0,1},{1,2},{2,3},{3,4},{4,5},{5,6},{6,7},{8,9},{9,10},{10,11},{11... | collective-permute-start | bytes 59912 | tf_op jit(solution)/shard_map/ppermute | solution.py:15
  24.3 34.0 %collective-permute-start.3 = (bf16[2,3,13,128]{3,2,1,0:T(8,128)(2,1)S(1)}, bf16[2,3,13,128]{3,2,1,0:T(8,128)(2,1)S(1)}, u32[]{:S(2)}, u32[]{:S(2)}) collective-permute-start(bf16[2,3,13,128]{3,2,1,0:T(8,128)(2,1)S(1)} %get-tuple-element.1179), channel_id=1, source_target_pairs={{1,0},{2,1},{3,2},{4,3},{5,4},{6,5},{7,6},{9,8},{10,9},{11,10},{12... | collective-permute-start | bytes 59912 | tf_op jit(solution)/shard_map/ppermute | solution.py:17
  26.6 16.7 %collective-permute-start = (bf16[64,1,128]{2,1,0:T(2,128)(2,1)S(1)}, bf16[64,1,128]{2,1,0:T(2,128)(2,1)S(1)}, u32[]{:S(2)}, u32[]{:S(2)}) collective-permute-start(bf16[64,1,128]{2,1,0:T(2,128)(2,1)S(1)} %get-tuple-element.1172), channel_id=1, source_target_pairs={{0,1},{1,2},{2,3},{3,4},{4,5},{5,6},{6,7},{8,9},{9,10},{10,11},{11... | collective-permute-start | bytes 49160 | tf_op jit(solution)/shard_map/ppermute | solution.py:15
  39.4 13.4 %collective-permute-start.1 = (bf16[64,1,128]{2,1,0:T(2,128)(2,1)S(1)}, bf16[64,1,128]{2,1,0:T(2,128)(2,1)S(1)}, u32[]{:S(2)}, u32[]{:S(2)}) collective-permute-start(bf16[64,1,128]{2,1,0:T(2,128)(2,1)S(1)} %get-tuple-element.1173), channel_id=1, source_target_pairs={{1,0},{2,1},{3,2},{4,3},{5,4},{6,5},{7,6},{9,8},{10,9},{11,10},{12... | collective-permute-start | bytes 49160 | tf_op jit(solution)/shard_map/ppermute | solution.py:17
  43.4 11.6 %copy-start.6 = (bf16[1,64,16,128]{3,2,1,0:T(8,128)(2,1)S(1)}, bf16[1,64,16,128]{3,2,1,0:T(8,128)(2,1)}, u32[]{:S(2)}) copy-start(bf16[1,64,16,128]{3,2,1,0:T(8,128)(2,1)} %param.35) | copy-start | bytes 786436
  120.0 131.0 %copy-start.3 = (bf16[576,2048]{1,0:T(8,128)(2,1)S(1)}, bf16[576,2048]{1,0:T(8,128)(2,1)}, u32[]{:S(2)}) copy-start(bf16[576,2048]{1,0:T(8,128)(2,1)} %copy-done.2) | copy-start | bytes 7077892
  129.2 3.5 copy-start.7
  130.1 2.6 copy-start.8
  143.5 3.5 copy-start.7
  144.4 2.6 copy-start.8
  157.8 3.5 copy-start.7
  158.7 2.6 copy-start.8
  172.2 3.5 copy-start.7
  186.5 3.5 copy-start.7
  200.8 3.5 copy-start.7
  215.1 3.5 copy-start.7
  215.9 2.6 copy-start.8
  229.4 3.5 copy-start.7
  230.2 2.6 copy-start.8
  243.7 3.4 copy-start.7
  250.2 3.5 copy-start.11
  250.2 3.5 copy-start.12
  274.9 8.0 %copy-start.9 = (f32[8,16,8,128]{3,2,1,0:T(8,128)S(1)}, f32[8,16,8,128]{3,2,1,0:T(8,128)}, u32[]{:S(2)}) copy-start(f32[8,16,8,128]{3,2,1,0:T(8,128)} %get-tuple-element.1152) | copy-start | bytes 1572868
  288.7 12.3 %copy-start.10 = (f32[1,3,42,128]{3,2,1,0:T(8,128)S(1)}, f32[1,3,42,128]{3,2,1,0:T(8,128)}, u32[]{:S(2)}) copy-start(f32[1,3,42,128]{3,2,1,0:T(8,128)} %slice_bitcast_fusion.64) | copy-start | bytes 193540
  296.9 16.8 %collective-permute-start.4 = (f32[64,1,128]{2,0,1:T(8,128)S(1)}, f32[64,1,128]{2,0,1:T(8,128)S(1)}, u32[]{:S(2)}, u32[]{:S(2)}) collective-permute-start(f32[64,1,128]{2,0,1:T(8,128)S(1)} %get-tuple-element.1159), channel_id=1, source_target_pairs={{0,1},{1,2},{2,3},{3,4},{4,5},{5,6},{6,7},{8,9},{9,10},{10,11},{11... | collective-permute-start | bytes 98312 | tf_op jit(solution)/shard_map/ppermute | solution.py:27
  301.2 12.6 %collective-permute-start.6 = (f32[2,3,13,128]{3,2,1,0:T(8,128)S(1)}, f32[2,3,13,128]{3,2,1,0:T(8,128)S(1)}, u32[]{:S(2)}, u32[]{:S(2)}) collective-permute-start(f32[2,3,13,128]{3,2,1,0:T(8,128)S(1)} %fusion.19), channel_id=1, source_target_pairs={{0,1},{1,2},{2,3},{3,4},{4,5},{5,6},{6,7},{8,9},{9,10},{10,11},{11... | collective-permute-start | bytes 119816 | tf_op jit(solution)/shard_map/ppermute | solution.py:27
  312.4 13.9 %collective-permute-start.5 = (f32[64,1,128]{2,0,1:T(8,128)S(1)}, f32[64,1,128]{2,0,1:T(8,128)S(1)}, u32[]{:S(2)}, u32[]{:S(2)}) collective-permute-start(f32[64,1,128]{2,0,1:T(8,128)S(1)} %get-tuple-element.1158), channel_id=1, source_target_pairs={{1,0},{2,1},{3,2},{4,3},{5,4},{6,5},{7,6},{9,8},{10,9},{11,10},{12... | collective-permute-start | bytes 98312 | tf_op jit(solution)/shard_map/ppermute | solution.py:27
  313.8 14.3 %collective-permute-start.7 = (f32[2,3,13,128]{3,2,1,0:T(8,128)S(1)}, f32[2,3,13,128]{3,2,1,0:T(8,128)S(1)}, u32[]{:S(2)}, u32[]{:S(2)}) collective-permute-start(f32[2,3,13,128]{3,2,1,0:T(8,128)S(1)} %get-tuple-element.1174), channel_id=1, source_target_pairs={{1,0},{2,1},{3,2},{4,3},{5,4},{6,5},{7,6},{9,8},{10,9},{11,10},{12... | collective-permute-start | bytes 119816 | tf_op jit(solution)/shard_map/ppermute | solution.py:27
  326.8 449.0 %copy-start.15 = (f32[1,64,16,128]{3,2,1,0:T(8,128)}, f32[1,64,16,128]{3,2,1,0:T(8,128)S(1)}, u32[]{:S(2)}) copy-start(f32[1,64,16,128]{3,2,1,0:T(8,128)S(1)} %scatter-add.60) | copy-start | bytes 1572868
  328.3 447.5 %copy-start.17 = (f32[1,2,3,16,128]{4,3,2,1,0:T(8,128)}, f32[1,2,3,16,128]{4,3,2,1,0:T(8,128)S(1)}, u32[]{:S(2)}) copy-start(f32[1,2,3,16,128]{4,3,2,1,0:T(8,128)S(1)} %scatter-add.64) | copy-start | bytes 147460
  (11 other events, 19.8 us)
Sparse Core Ops, SparseCore 0:
  312.5 461.5 all-reduce.167
where the time goes:
time: 785 us; the launch traced here: 783 us
  waiting for transfers between devices  468 us (60%)
  other arithmetic  145 us (18%)
  local copies, waits for them, and re-layouts  86.8 us (11%)
  starting transfers between devices  49.4 us (6%)
  between operations  14.7 us (2%)
  loops' own time  14.3 us (2%)
    psum x1, waiting for transfers between devices, shards(): weight_sum = lax.psum(weight_part, ('dp', 'tile'))  446 us
    add x54, other arithmetic, one_tap(): old_rows + back_sum  41.1 us
    reduce_sum x72, other arithmetic, one_tap(): horiz_rows.append(jnp.sum(scaled * shifted, 0))  29.5 us
    mul x90, other arithmetic, one_tap(): weight_row * scaled  29.3 us
    ppermute x2, starting transfers between devices, with_halo(): lax.ppermute(tail, axis, [(i, (i + 1) % count) for i in range(ends)])  29 us
    scatter-add x7, local copies, waits for them, and re-layouts, fold_patches(): folded = folded.at[:, row_shift:row_shift + row_count, col_shift:col_shif...  28.3 us
    reduce_sum x54, other arithmetic, one_tap(): jnp.sum(upstream * blended, 0)[None]  25.7 us
    ppermute x4, starting transfers between devices, from_behind(): lax.ppermute(value, axis, [(source, source + steps) for source in range(l...  17.8 us
  transfers between devices with their start and end apart: 9, of which 4 were waited for; matrix products, arithmetic and copies ran while one was open for 1% of the time, Pallas kernels for 0%

commit v1 on v0

v1 whole, which is shorter than its diff:
```python
import functools
import jax
import jax.numpy as jnp
from jax import lax
from jax.experimental import pallas as pl
from jax.experimental.pallas import tpu as pltpu
from jax.sharding import Mesh, PartitionSpec as P

F32, BF16 = jnp.float32, jnp.bfloat16
UNROLL = 4


def dims(a, b):
    return (((a,), (b,)), ((), ()))


def split(v):
    hi = v.astype(BF16)
    lo = (v - hi.astype(F32)).astype(BF16)
    return hi, lo


def row_kernel(taps, feat, halo_up, halo_dn, frames, cot, wfwd, wbwd,
               parts_ref, gfeat, gframe, rim_up, rim_dn,
               fs, fb, ip, gf, acc, wg, flat):
    rim = (taps - 1) // 2
    channels, rows, width = feat.shape
    scale = taps ** -0.5
    lane = lax.broadcasted_iota(jnp.int32, (width, width), 1)
    sub = lax.broadcasted_iota(jnp.int32, (width, width), 0)
    first, last = lane[:channels] == 0, lane[:channels] == width - 1

    fs[...] = feat[...].astype(F32).reshape(channels * rows, width)

    def put(at, row):
        left = jnp.where(first, 0.0, pltpu.roll(row, 1, 1))
        right = jnp.where(last, 0.0, pltpu.roll(row, width - 1, 1))
        fb[at] = jnp.concatenate([left, row, right], 0).astype(BF16)

    put(0, halo_up[:channels].astype(F32))
    put(rows + 1, halo_dn[:channels].astype(F32))
    for y in range(rows):
        put(y + 1, fs[pl.ds(y, channels, stride=rows), :])

    for n in range(6):
        f, c = divmod(n, 3)
        at = channels + n * rim
        turn = rim + 64 * f
        ip[n] = jnp.zeros(ip.shape[1:], F32)
        ip[n, :rim] = halo_up[at:at + rim].astype(F32)
        ip[n, rim:rim + rows] = frames[f, c].astype(F32)
        ip[n, rim + rows:rim + rows + rim] = halo_dn[at:at + rim].astype(F32)
        ip[n] = pltpu.roll(ip[n], turn, 1)
    gf[...] = jnp.zeros_like(gf)
    acc[...] = jnp.zeros_like(acc)
    wg[...] = jnp.zeros_like(wg)

    bands = []
    for f in range(2):
        tap = (lane - sub + (2 * width - 64 * f)) % width
        at = sub + tap - rim
        bands.append((tap < taps) & (at >= 0) & (at < width))

    def step(y, carry):
        patches = fb[pl.ds(y, 3)].reshape(9 * channels, width)
        k = jnp.dot(wfwd[...], patches, preferred_element_type=F32) * scale
        skew = pltpu.roll(k.T, 0, 1, stride=1, stride_axis=0)
        g = [cot[c, pl.ds(y, 1), :] for c in range(3)]
        grads = []
        horiz = None
        for f in range(2):
            v = k[64 * f + 32:64 * f + 64]
            u = jnp.concatenate([v * g[c] for c in range(3)], 0)
            window = jnp.concatenate(
                [ip[3 * f + c, pl.ds(y, 32), :] for c in range(3)], 0).astype(BF16)
            b = jnp.where(bands[f], skew, 0.0)
            b_hi, b_lo = split(b)
            u_hi, u_lo = split(u)
            blended = lax.dot_general(
                jnp.concatenate([window, window], 1), jnp.concatenate([b_hi, b_lo], 1),
                dims(1, 1), preferred_element_type=F32)
            grads.append(sum(g[c] * blended[32 * c:32 * c + 32] for c in range(3)))
            d = lax.dot_general(
                jnp.concatenate([u_hi, u_lo], 0), jnp.concatenate([window, window], 0),
                dims(0, 0), preferred_element_type=F32)
            horiz = jnp.where(bands[0], d, 0.0) if f == 0 else jnp.where(bands[1], d, horiz)
            w = jnp.dot(
                jnp.concatenate([u_hi, u_hi, u_lo], 1),
                jnp.concatenate([b_hi, b_lo, b_hi], 0), preferred_element_type=F32)
            for c in range(3):
                gf[3 * f + c, pl.ds(y, 32), :] += w[32 * c:32 * c + 32]
        parts = []
        for r in range(width // 8):
            p = horiz[8 * r:8 * r + 8]
            if r:
                p = pltpu.roll(p, width - 8 * r, 1)
            parts.append(p)
        horiz = jnp.concatenate(parts, 0)
        for bit in range(3):
            horiz = jnp.where((sub & (1 << bit)) != 0, pltpu.roll(horiz, width - (1 << bit), 1), horiz)
        ht = horiz.T
        kg = jnp.concatenate([ht[:32], grads[0], ht[64:96], grads[1]], 0) * scale
        kgb = kg.astype(BF16)
        wg[...] += lax.dot_general(kgb, patches, dims(1, 1), preferred_element_type=F32)
        kgr = kgb.astype(F32)
        wide = jnp.concatenate([
            jnp.where(lane == width - 1, 0.0, pltpu.roll(kgr, width - 1, 1)),
            kgr,
            jnp.where(lane == 0, 0.0, pltpu.roll(kgr, 1, 1))], 0).astype(BF16)
        part = jnp.dot(wbwd[...], wide, preferred_element_type=F32)
        for a in range(3):
            acc[y + a] += part[channels * a:channels * (a + 1)]
        return carry

    lax.fori_loop(0, rows, step, 0, unroll=UNROLL)

    for y in range(rows):
        gfeat[pl.ds(y, channels, stride=rows), :] = acc[y + 1]
    rim_up[:channels] = acc[0].astype(BF16)
    rim_dn[:channels] = acc[rows + 1].astype(BF16)
    for n in range(6):
        gf[n] = pltpu.roll(gf[n], width - rim - 64 * (n // 3), 1)
        gframe[n] = gf[n, rim:rim + rows]
        at = channels + n * rim
        rim_up[at:at + rim] = gf[n, :rim].astype(BF16)
        rim_dn[at:at + rim] = gf[n, rim + rows:rim + rows + rim].astype(BF16)
    pack(wg[...], flat)
    count, size = parts_ref.shape[:2]
    for n in range(count):
        parts_ref[n] = flat[size * n:size * (n + 1)]


def pack(value, flat):
    full = value.shape[1] // 128
    for n in range(full):
        flat[128 * n:128 * (n + 1)] = value[:, 128 * n:128 * (n + 1)]
    tail = value[:, 128 * full:]
    flat[128 * full:] = jnp.concatenate([tail[:64], tail[64:]], 1)


def unpack_kernel(taps, factor, parts_ref, out, flat):
    count, size = parts_ref.shape[:2]
    for n in range(count):
        flat[size * n:size * (n + 1)] = parts_ref[n]
    full = out.shape[1] // 128
    tail = flat[128 * full:]
    blocks = [flat[128 * n:128 * (n + 1)] for n in range(full)]
    blocks.append(jnp.concatenate([tail[:, :64], tail[:, 64:]], 0))
    value = jnp.concatenate(blocks, 1) * factor
    for n, group in enumerate((1, 0, 3, 2)):
        out[taps * n:taps * (n + 1)] = value[32 * group:32 * group + taps]


def order(hw, taps):
    hw = hw.reshape(2, 2, taps, -1)[:, ::-1]
    return jnp.pad(hw, ((0, 0), (0, 0), (0, 32 - taps), (0, 0))).reshape(128, -1)


def local_grads(feat, halo_up, halo_dn, frames, cot, hw, parts):
    channels, rows, width = feat.shape
    taps = hw.shape[0] // 4
    rim = (taps - 1) // 2
    columns = 9 * channels
    wfwd = order(hw, taps)
    wbwd = wfwd.reshape(128, 3, 3, channels).transpose(1, 3, 2, 0).reshape(3 * channels, 3 * 128)
    vm = pl.BlockSpec(memory_space=pltpu.VMEM)
    return pl.pallas_call(
        functools.partial(row_kernel, taps),
        out_shape=(
            jax.ShapeDtypeStruct((parts, columns // parts, 128), F32),
            jax.ShapeDtypeStruct((channels * rows, width), F32),
            jax.ShapeDtypeStruct((6, rows, width), F32),
            jax.ShapeDtypeStruct((channels + 6 * rim, width), BF16),
            jax.ShapeDtypeStruct((channels + 6 * rim, width), BF16),
        ),
        in_specs=[vm] * 7,
        out_specs=[vm] * 5,
        scratch_shapes=[
            pltpu.VMEM((channels * rows, width), F32),
            pltpu.VMEM((rows + 2, 3 * channels, width), BF16),
            pltpu.VMEM((6, rows + 32, width), F32),
            pltpu.VMEM((6, rows + 32, width), F32),
            pltpu.VMEM((rows + 2, channels, width), F32),
            pltpu.VMEM((128, columns), F32),
            pltpu.VMEM((columns, 128), F32),
        ],
    )(feat, halo_up, halo_dn, frames, cot, wfwd, wbwd)


def unpack(parts, taps, factor):
    count, size, _ = parts.shape
    vm = pl.BlockSpec(memory_space=pltpu.VMEM)
    return pl.pallas_call(
        functools.partial(unpack_kernel, taps, factor),
        out_shape=jax.ShapeDtypeStruct((4 * taps, count * size), F32),
        in_specs=[vm],
        out_specs=vm,
        scratch_shapes=[pltpu.VMEM((count * size, 128), F32)],
    )(parts)


PLANE, LINE, TILE = ("y", "core", "x"), ("zl", "zh"), ("x", "zh")


def spread(value, axes, count):
    return lax.all_to_all(jnp.broadcast_to(value[None], (count,) + value.shape), axes, 0, 0)


def shards(frames, features, cotangent, head_weight):
    taps = head_weight.shape[0] // 4
    rim = (taps - 1) // 2
    feat, frame, cot = features[0], frames[0], cotangent[0]
    channels, rows, width = feat.shape
    tiles, plane, line = lax.axis_size(TILE), lax.axis_size(PLANE), lax.axis_size(LINE)
    down = [(i, i + 1) for i in range(tiles - 1)]
    up = [(i + 1, i) for i in range(tiles - 1)]

    def halo(row, part):
        return jnp.concatenate([feat[:, row], part.reshape(6 * rim, width)], 0)

    halo_up = lax.ppermute(halo(rows - 1, frame[:, :, rows - rim:]), TILE, down)
    halo_dn = lax.ppermute(halo(0, frame[:, :, :rim]), TILE, up)
    parts, gfeat, gframe, rim_up, rim_dn = local_grads(
        feat, halo_up, halo_dn, frame, cot, head_weight, plane)

    from_up = lax.ppermute(rim_dn, TILE, down).astype(F32)
    from_dn = lax.ppermute(rim_up, TILE, up).astype(F32)

    own = jnp.sum(lax.all_to_all(parts, PLANE, 0, 0), 0)
    own = jnp.sum(spread(own, LINE, line), 0)
    total = spread(own, PLANE, plane)
    pixels = plane * line * rows * width
    grad_weight = unpack(total, taps, pixels ** -0.5)

    gfeat = gfeat.reshape(channels, rows, width)
    gfeat = (gfeat + jnp.pad(from_up[:channels, None], ((0, 0), (0, rows - 1), (0, 0)))
             + jnp.pad(from_dn[:channels, None], ((0, 0), (rows - 1, 0), (0, 0))))
    gframe = (gframe
              + jnp.pad(from_up[channels:].reshape(6, rim, width), ((0, 0), (0, rows - rim), (0, 0)))
              + jnp.pad(from_dn[channels:].reshape(6, rim, width), ((0, 0), (rows - rim, 0), (0, 0))))
    return grad_weight, gfeat[None], gframe.reshape(1, 2, 3, rows, width)


def solution(mesh):
    fine = Mesh(mesh.devices.reshape(8, 4, 2, 4, 2), ("zl", "y", "core", "x", "zh"))
    pairs, tile = ("zl", "y", "core"), ("x", "zh")
    in_specs = (
        P(pairs, None, None, tile, None),
        P(pairs, None, tile, None),
        P(pairs, None, tile, None),
        P(),
    )
    out_specs = (P(), P(pairs, None, tile, None), P(pairs, None, None, tile, None))
    return jax.shard_map(shards, mesh=fine, in_specs=in_specs, out_specs=out_specs, check_vma=False)
```

time: 785 us -> 124 us (0.16)
  waiting for transfers between devices: 468 us -> 30.7 us
  other arithmetic: 145 us -> 0.9 us
  local copies, waits for them, and re-layouts: 86.8 us -> 7.54 us
  Pallas kernels: 0 us -> 21.3 us
  blocking collectives: 0 us -> 21.2 us
  loops' own time: 14.3 us -> 0 us
  between operations: 14.7 us -> 0.91 us
  starting transfers between devices: 49.4 us -> 40.6 us
    psum x1 -> x0, waiting for transfers between devices: 446 us -> none  [shards(): weight_sum = lax.psum(weight_part, ('dp', 'tile'))]
    reduce_sum x126 -> x2, other arithmetic: 55.2 us -> 0.06 us  [the longest x1 0.04 us: shards(): own = jnp.sum(lax.all_to_all(parts, PLANE, 0, 0), 0)]
    add x78 -> x1, other arithmetic: 50.5 us -> 0.63 us  [shards(): gframe + jnp.pad(from_up[channels:].reshape(6, rim, width), ((0, 0), (0,...]
    dynamic_update_slice x108 -> x0, local copies, waits for them, and re-layouts: 33 us -> none  [the longest x54 16.6 us: one_tap(): lax.dynamic_update_slice_in_dim(grad_padded, old_rows + back_sum, tap_ind...]
    mul x92 -> x0, other arithmetic: 31.1 us -> none  [the longest x90 29.3 us: one_tap(): weight_row * scaled]
    scatter-add x10 -> x0, local copies, waits for them, and re-layouts: 28.8 us -> none  [the longest x7 28.3 us: fold_patches(): folded = folded.at[:, row_shift:row_shift + row_count, col_shift:col_shif...]
    pallas_call x0 -> x2, Pallas kernels: none -> 21.3 us  [the longest x1 19.5 us: local_grads(): pl.pallas_call(functools.partial(row_kernel, taps), out_shape=(jax.ShapeD...]
    all_to_all x0 -> x1, blocking collectives: none -> 21.2 us  [shards(): own = jnp.sum(lax.all_to_all(parts, PLANE, 0, 0), 0)]
  transfers between devices with their start and end apart: 9 -> 6, of which waited for: 4 -> 3; matrix products, arithmetic and copies ran while one was open for 1% -> 3% of each run, Pallas kernels for 0% -> 0%
where the time goes in v1:
time: 124 us; the launch traced here: 123 us
  starting transfers between devices  40.6 us (33%)
  waiting for transfers between devices  30.7 us (25%)
  Pallas kernels  21.3 us (17%)
  blocking collectives  21.2 us (17%)
  local copies, waits for them, and re-layouts  7.54 us (6%)
    all_to_all x1, blocking collectives, shards(): own = jnp.sum(lax.all_to_all(parts, PLANE, 0, 0), 0)  21.2 us
    pallas_call x1, Pallas kernels, local_grads(): pl.pallas_call(functools.partial(row_kernel, taps), out_shape=(jax.ShapeD...  19.5 us
    ppermute x1, starting transfers between devices, shards(): halo_up = lax.ppermute(halo(rows - 1, frame[:, :, rows - rim:]), TILE, down)  16.4 us
    ppermute x1, waiting for transfers between devices, shards(): from_dn = lax.ppermute(rim_up, TILE, up).astype(F32)  12.1 us
    ppermute x1, starting transfers between devices, shards(): from_up = lax.ppermute(rim_dn, TILE, down).astype(F32)  11.9 us
    ppermute x1, waiting for transfers between devices, shards(): halo_dn = lax.ppermute(halo(0, frame[:, :, :rim]), TILE, up)  10.4 us
    all_to_all x2, starting transfers between devices, spread(): lax.all_to_all(jnp.broadcast_to(value[None], (count,) + value.shape), axe...  9.75 us
    all_to_all x2, waiting for transfers between devices, spread(): lax.all_to_all(jnp.broadcast_to(value[None], (count,) + value.shape), axe...  8.16 us
  transfers between devices with their start and end apart: 6, of which 3 were waited for; matrix products, arithmetic and copies ran while one was open for 3% of the time, Pallas kernels for 0%

profile of v1, /device:TPU:1, one launch (start us, length us, event | category | flops | bytes accessed | tf_op | source)
XLA Modules:
  0.0 123.1 jit_solution(3844166866863790618)
XLA Ops:
  0.6 0.8 fusion.2
  1.5 1.0 copy.36
  2.5 0.0 copy-start.3
  2.5 16.4 %collective-permute-start = (bf16[142,128]{1,0:T(8,128)(2,1)S(1)}, bf16[142,128]{1,0:T(8,128)(2,1)S(1)}, u32[]{:S(2)}, u32[]{:S(2)}) collective-permute-start(bf16[142,128]{1,0:T(8,128)(2,1)S(1)} %pad_maximum_fusion), channel_id=1, source_target_pairs={{0,1},{1,2},{2,3},{3,4},{4,5},{5,6},{6,7},{8,9},{9,10},{10,11},{11... | collective-permute-start | bytes 109064 | tf_op jit(solution)/shard_map/ppermute | solution.py:221
  19.0 1.3 %collective-permute-start.1 = (bf16[142,128]{1,0:T(8,128)(2,1)S(1)}, bf16[142,128]{1,0:T(8,128)(2,1)S(1)}, u32[]{:S(2)}, u32[]{:S(2)}) collective-permute-start(bf16[142,128]{1,0:T(8,128)(2,1)S(1)} %pad_maximum_fusion.1), channel_id=1, source_target_pairs={{1,0},{2,1},{3,2},{4,3},{5,4},{6,5},{7,6},{9,8},{10,9},{11,10},{12... | collective-permute-start | bytes 109064 | tf_op jit(solution)/shard_map/ppermute | solution.py:222
  20.3 0.1 reshape.37
  20.4 0.0 copy-start.1
  20.4 0.2 reshape_reshape.3
  20.7 0.4 copy-done.1
  21.1 0.3 copy.21
  21.3 0.7 copy.37
  22.0 0.0 collective-permute-done.halo_up
  22.0 10.4 %collective-permute-done.1.halo_dn = bf16[142,128]{1,0:T(8,128)(2,1)S(1)} collective-permute-done((bf16[142,128]{1,0:T(8,128)(2,1)S(1)}, bf16[142,128]{1,0:T(8,128)(2,1)S(1)}, u32[]{:S(2)}, u32[]{:S(2)}) %collective-permute-start.1) | collective-permute-done | bytes 36384 | tf_op jit(solution)/shard_map/ppermute | solution.py:222
  32.4 0.6 copy-done.6
  33.0 19.5 %shard_map.67 = (f32[32,18,128]{2,1,0:T(8,128)}, f32[1024,128]{1,0:T(8,128)}, f32[6,16,128]{2,1,0:T(8,128)}, bf16[142,128]{1,0:T(8,128)(2,1)}, bf16[142,128]{1,0:T(8,128)(2,1)}) custom-call(bf16[64,16,128]{2,1,0:T(8,128)(2,1)} %bitcast.29, bf16[142,128]{1,0:T(8,128)(2,1)} %copy-done.5, bf16[142,128]{1,0:T(8,128)(2,1)} %copy-done.6, ...), custom_call_target="tpu_custom_call" | custom-call | tf_op jit(solution)/shard_map/pallas_call | solution.py:167
  52.5 21.2 %all_to_all.15 = f32[32,18,128]{2,1,0:T(8,128)S(1)} all-to-all(f32[32,18,128]{2,1,0:T(8,128)} %get-tuple-element.8), channel_id=1, replica_groups=mesh['zl'=8,'y'=4,'core'=2,'x'=4,'zh'=2] {'y','core','x'}, dimensions={0} | all-to-all | bytes 589824 | tf_op jit(solution)/shard_map/all_to_all | solution.py:229
  73.8 0.7 broadcast_in_dim.10
  74.5 3.7 %all-to-all-start.1 = ((f32[16,18,128]{2,1,0:T(8,128)}), f32[16,18,128]{2,1,0:T(8,128)S(1)}, u32[]{:S(2)}, u32[]{:S(2)}) async-start(f32[16,18,128]{2,1,0:T(8,128)} %broadcast_in_dim.10), calls=%async_computation.1 | async-start | bytes 393216 | tf_op jit(solution)/shard_map/all_to_all | solution.py:206
  78.1 11.9 %collective-permute-start.2 = (bf16[142,128]{1,0:T(8,128)(2,1)S(1)}, bf16[142,128]{1,0:T(8,128)(2,1)S(1)}, u32[]{:S(2)}, u32[]{:S(2)}) collective-permute-start(bf16[142,128]{1,0:T(8,128)(2,1)S(1)} %copy-done.8), channel_id=1, source_target_pairs={{0,1},{1,2},{2,3},{3,4},{4,5},{5,6},{6,7},{8,9},{9,10},{10,11},{11... | collective-permute-start | bytes 109064 | tf_op jit(solution)/shard_map/ppermute | solution.py:226
  90.0 1.3 %collective-permute-start.3 = (bf16[142,128]{1,0:T(8,128)(2,1)S(1)}, bf16[142,128]{1,0:T(8,128)(2,1)S(1)}, u32[]{:S(2)}, u32[]{:S(2)}) collective-permute-start(bf16[142,128]{1,0:T(8,128)(2,1)S(1)} %copy-done.7), channel_id=1, source_target_pairs={{1,0},{2,1},{3,2},{4,3},{5,4},{6,5},{7,6},{9,8},{10,9},{11,10},{12... | collective-permute-start | bytes 109064 | tf_op jit(solution)/shard_map/ppermute | solution.py:227
  91.3 0.0 collective-permute-done.2
  91.4 12.1 %collective-permute-done.3 = bf16[142,128]{1,0:T(8,128)(2,1)S(1)} collective-permute-done((bf16[142,128]{1,0:T(8,128)(2,1)S(1)}, bf16[142,128]{1,0:T(8,128)(2,1)S(1)}, u32[]{:S(2)}, u32[]{:S(2)}) %collective-permute-start.3) | collective-permute-done | bytes 36384 | tf_op jit(solution)/shard_map/ppermute | solution.py:227
  103.6 0.0 copy-start.2
  103.6 0.8 broadcast_in_dim.22
  104.3 6.1 %all-to-all-start.2 = ((f32[32,18,128]{2,1,0:T(8,128)}), f32[32,18,128]{2,1,0:T(8,128)S(1)}, u32[]{:S(2)}, u32[]{:S(2)}) async-start(f32[32,18,128]{2,1,0:T(8,128)} %broadcast_in_dim.22), calls=%async_computation.2 | async-start | bytes 786432 | tf_op jit(solution)/shard_map/all_to_all | solution.py:206
  110.5 0.2 fusion.1
  110.7 0.0 copy-start.4
  110.7 1.1 copy.25
  111.8 0.6 pad_add_fusion
  112.4 8.2 %all-to-all-done.2.parts_ref = f32[32,18,128]{2,1,0:T(8,128)S(1)} async-done(((f32[32,18,128]{2,1,0:T(8,128)}), f32[32,18,128]{2,1,0:T(8,128)S(1)}, u32[]{:S(2)}, u32[]{:S(2)}) %all-to-all-start.2) | async-done | bytes 294944 | tf_op jit(solution)/shard_map/all_to_all | solution.py:206
  120.6 0.7 copy-done
  121.3 1.8 %shard_map.68 = f32[108,576]{1,0:T(8,128)} custom-call(f32[32,18,128]{2,1,0:T(8,128)} %copy-done), custom_call_target="tpu_custom_call" | custom-call | tf_op jit(solution)/shard_map/pallas_call | solution.py:193
  (29 shorter events, 0.2 us)
Async XLA Ops:
  2.5 17.8 %copy-start.3 = (bf16[108,576]{1,0:T(8,128)(2,1)S(1)}, bf16[108,576]{1,0:T(8,128)(2,1)}, u32[]{:S(2)}) copy-start(bf16[108,576]{1,0:T(8,128)(2,1)} %param.7) | copy-start | bytes 373252
  2.5 19.5 %collective-permute-start = (bf16[142,128]{1,0:T(8,128)(2,1)S(1)}, bf16[142,128]{1,0:T(8,128)(2,1)S(1)}, u32[]{:S(2)}, u32[]{:S(2)}) collective-permute-start(bf16[142,128]{1,0:T(8,128)(2,1)S(1)} %pad_maximum_fusion), channel_id=1, source_target_pairs={{0,1},{1,2},{2,3},{3,4},{4,5},{5,6},{6,7},{8,9},{9,10},{10,11},{11... | collective-permute-start | bytes 109064 | tf_op jit(solution)/shard_map/ppermute | solution.py:221
  19.0 13.4 %collective-permute-start.1 = (bf16[142,128]{1,0:T(8,128)(2,1)S(1)}, bf16[142,128]{1,0:T(8,128)(2,1)S(1)}, u32[]{:S(2)}, u32[]{:S(2)}) collective-permute-start(bf16[142,128]{1,0:T(8,128)(2,1)S(1)} %pad_maximum_fusion.1), channel_id=1, source_target_pairs={{1,0},{2,1},{3,2},{4,3},{5,4},{6,5},{7,6},{9,8},{10,9},{11,10},{12... | collective-permute-start | bytes 109064 | tf_op jit(solution)/shard_map/ppermute | solution.py:222
  20.4 0.7 copy-start.1
  22.0 10.4 %copy-start.5 = (bf16[142,128]{1,0:T(8,128)(2,1)}, bf16[142,128]{1,0:T(8,128)(2,1)S(1)}, u32[]{:S(2)}) copy-start(bf16[142,128]{1,0:T(8,128)(2,1)S(1)} %collective-permute-done.halo_up) | copy-start | bytes 109060
  32.4 0.6 copy-start.6
  74.5 3.7 %copy-start.8 = (bf16[142,128]{1,0:T(8,128)(2,1)S(1)}, bf16[142,128]{1,0:T(8,128)(2,1)}, u32[]{:S(2)}) copy-start(bf16[142,128]{1,0:T(8,128)(2,1)} %get-tuple-element.10) | copy-start | bytes 109060
  74.5 15.5 %copy-start.7 = (bf16[142,128]{1,0:T(8,128)(2,1)S(1)}, bf16[142,128]{1,0:T(8,128)(2,1)}, u32[]{:S(2)}) copy-start(bf16[142,128]{1,0:T(8,128)(2,1)} %get-tuple-element.11) | copy-start | bytes 109060
  74.5 29.0 %all-to-all-start.1 = ((f32[16,18,128]{2,1,0:T(8,128)}), f32[16,18,128]{2,1,0:T(8,128)S(1)}, u32[]{:S(2)}, u32[]{:S(2)}) async-start(f32[16,18,128]{2,1,0:T(8,128)} %broadcast_in_dim.10), calls=%async_computation.1 | async-start | bytes 393216 | tf_op jit(solution)/shard_map/all_to_all | solution.py:206
  78.1 13.2 %collective-permute-start.2 = (bf16[142,128]{1,0:T(8,128)(2,1)S(1)}, bf16[142,128]{1,0:T(8,128)(2,1)S(1)}, u32[]{:S(2)}, u32[]{:S(2)}) collective-permute-start(bf16[142,128]{1,0:T(8,128)(2,1)S(1)} %copy-done.8), channel_id=1, source_target_pairs={{0,1},{1,2},{2,3},{3,4},{4,5},{5,6},{6,7},{8,9},{9,10},{10,11},{11... | collective-permute-start | bytes 109064 | tf_op jit(solution)/shard_map/ppermute | solution.py:226
  90.0 13.5 %collective-permute-start.3 = (bf16[142,128]{1,0:T(8,128)(2,1)S(1)}, bf16[142,128]{1,0:T(8,128)(2,1)S(1)}, u32[]{:S(2)}, u32[]{:S(2)}) collective-permute-start(bf16[142,128]{1,0:T(8,128)(2,1)S(1)} %copy-done.7), channel_id=1, source_target_pairs={{1,0},{2,1},{3,2},{4,3},{5,4},{6,5},{7,6},{9,8},{10,9},{11,10},{12... | collective-permute-start | bytes 109064 | tf_op jit(solution)/shard_map/ppermute | solution.py:227
  103.6 6.9 %copy-start.2 = (f32[1024,128]{1,0:T(8,128)S(1)}, f32[1024,128]{1,0:T(8,128)}, u32[]{:S(2)}) copy-start(f32[1024,128]{1,0:T(8,128)} %get-tuple-element.9) | copy-start | bytes 1572868
  104.3 16.3 %all-to-all-start.2 = ((f32[32,18,128]{2,1,0:T(8,128)}), f32[32,18,128]{2,1,0:T(8,128)S(1)}, u32[]{:S(2)}, u32[]{:S(2)}) async-start(f32[32,18,128]{2,1,0:T(8,128)} %broadcast_in_dim.22), calls=%async_computation.2 | async-start | bytes 786432 | tf_op jit(solution)/shard_map/all_to_all | solution.py:206
  110.7 1.1 copy-start.4
  120.6 0.7 copy-start

commit v2 on v1

v2 whole, which is shorter than its diff:
```python
import functools
import jax
import jax.numpy as jnp
from jax import lax
from jax.experimental import pallas as pl
from jax.experimental.pallas import tpu as pltpu
from jax.sharding import Mesh, PartitionSpec as P


F32, BF16 = jnp.float32, jnp.bfloat16
UNROLL_EARLY = 7
UNROLL_LATE = 7
VMEM_GRANT = 16 * 1024 * 1024


def dims(a, b):
    return (((a,), (b,)), ((), ()))


def split(v):
    hi = v.astype(BF16)
    lo = (v - hi.astype(F32)).astype(BF16)
    return hi, lo


def column_bands(taps, width):
    rim = (taps - 1) // 2
    lane = lax.broadcasted_iota(jnp.int32, (width, width), 1)
    sub = lax.broadcasted_iota(jnp.int32, (width, width), 0)
    bands = []
    for f in range(2):
        tap = (lane - sub + (2 * width - 64 * f)) % width
        at = sub + tap - rim
        bands.append((tap < taps) & (at >= 0) & (at < width))
    return lane, sub, bands


def three_columns(row):
    lane = lax.broadcasted_iota(jnp.int32, row.shape, 1)
    width = row.shape[1]
    left = jnp.where(lane == 0, 0.0, pltpu.roll(row, 1, 1))
    right = jnp.where(lane == width - 1, 0.0, pltpu.roll(row, width - 1, 1))
    return jnp.concatenate([left, row, right], 0).astype(BF16)


def frame_terms(taps, k, g, bands):
    skew = pltpu.roll((k * taps ** -0.5).T, 0, 1, stride=1, stride_axis=0)
    out = []
    for f in range(2):
        v = k[64 * f + 32:64 * f + 64] * taps ** -0.5
        u_hi, u_lo = split(jnp.concatenate([v * g[c] for c in range(3)], 0))
        b_hi, b_lo = split(jnp.where(bands[f], skew, 0.0))
        w = jnp.dot(
            jnp.concatenate([u_hi, u_hi, u_lo], 1),
            jnp.concatenate([b_hi, b_lo, b_hi], 0), preferred_element_type=F32)
        out.append((jnp.concatenate([b_hi, b_lo], 1), jnp.concatenate([u_hi, u_lo], 0), w))
    return out


def early_kernel(taps, feat, cot, wfwd, fb, bst, ust, gf, fs):
    channels, rows, width = feat.shape
    fs[...] = feat[...].astype(F32).reshape(channels * rows, width)
    for y in range(rows):
        fb[y] = three_columns(fs[pl.ds(y, channels, stride=rows), :])
    gf[...] = jnp.zeros_like(gf)
    _, _, bands = column_bands(taps, width)

    def step(m, carry):
        ya = 2 * m + 1
        pair = jnp.concatenate(
            [fb[pl.ds(ya + h - 1, 3)].reshape(9 * channels, width) for h in range(2)], 1)
        k = jnp.dot(wfwd[...], pair, preferred_element_type=F32)
        for h in range(2):
            y = ya + h
            g = [cot[c, pl.ds(y, 1), :] for c in range(3)]
            terms = frame_terms(taps, k[:, width * h:width * (h + 1)], g, bands)
            for f, (b, u, w) in enumerate(terms):
                bst[y - 1, f] = b
                ust[y - 1, f] = u
                for c in range(3):
                    gf[3 * f + c, pl.ds(y, 32), :] += w[32 * c:32 * c + 32]
        return carry

    lax.fori_loop(0, rows // 2 - 1, step, 0, unroll=UNROLL_EARLY)


def late_kernel(taps, halo_up, halo_dn, frames, cot, wfwd, wbwd, fb, bst, ust, gf_in,
                parts_ref, gfeat, gframe, rim_up, rim_dn,
                ip, gf, acc, wg, flat):
    rim = (taps - 1) // 2
    rows, channels, width = fb.shape[0], fb.shape[1] // 3, fb.shape[2]
    lane, sub, bands = column_bands(taps, width)
    head = three_columns(halo_up[:channels].astype(F32))
    foot = three_columns(halo_dn[:channels].astype(F32))
    edges = jnp.concatenate([
        jnp.concatenate([head, fb[0], fb[1]], 0),
        jnp.concatenate([fb[rows - 2], fb[rows - 1], foot], 0)], 1)
    k = jnp.dot(wfwd[...], edges, preferred_element_type=F32)

    for n in range(6):
        f, c = divmod(n, 3)
        at = channels + n * rim
        ip[n] = jnp.zeros(ip.shape[1:], F32)
        ip[n, :rim] = halo_up[at:at + rim].astype(F32)
        ip[n, rim:rim + rows] = frames[f, c].astype(F32)
        ip[n, rim + rows:rim + rows + rim] = halo_dn[at:at + rim].astype(F32)
        ip[n] = pltpu.roll(ip[n], rim + 64 * f, 1)
    gf[...] = gf_in[...]
    acc[...] = jnp.zeros_like(acc)
    wg[...] = jnp.zeros_like(wg)

    def tap_grads(y, terms):
        g = [cot[c, pl.ds(y, 1), :] for c in range(3)]
        grads = []
        horiz = None
        for f, (b, u) in enumerate(terms):
            window = jnp.concatenate(
                [ip[3 * f + c, pl.ds(y, 32), :] for c in range(3)], 0).astype(BF16)
            blended = lax.dot_general(
                jnp.concatenate([window, window], 1), b, dims(1, 1), preferred_element_type=F32)
            grads.append(sum(g[c] * blended[32 * c:32 * c + 32] for c in range(3)))
            d = lax.dot_general(
                u, jnp.concatenate([window, window], 0), dims(0, 0), preferred_element_type=F32)
            horiz = jnp.where(bands[f], d, 0.0 if f == 0 else horiz)
        turned = [horiz[:8]]
        for r in range(1, width // 8):
            turned.append(pltpu.roll(horiz[8 * r:8 * r + 8], width - 8 * r, 1))
        horiz = jnp.concatenate(turned, 0)
        for bit in range(3):
            horiz = jnp.where((sub & (1 << bit)) != 0, pltpu.roll(horiz, width - (1 << bit), 1), horiz)
        ht = horiz.T
        kg = jnp.concatenate([ht[:32], grads[0], ht[64:96], grads[1]], 0) * taps ** -0.5
        return kg.astype(BF16)

    def accumulate(ya, yb, pair, kga, kgb):
        wg[...] += lax.dot_general(
            jnp.concatenate([kga, kgb], 1), pair, dims(1, 1), preferred_element_type=F32)
        wide = []
        for kg in (kga, kgb):
            kgr = kg.astype(F32)
            wide.append(jnp.concatenate([
                jnp.where(lane == width - 1, 0.0, pltpu.roll(kgr, width - 1, 1)),
                kgr,
                jnp.where(lane == 0, 0.0, pltpu.roll(kgr, 1, 1))], 0).astype(BF16))
        part = jnp.dot(wbwd[...], jnp.concatenate(wide, 1), preferred_element_type=F32)
        for a in range(3):
            acc[ya + a] += part[channels * a:channels * (a + 1), :width]
            acc[yb + a] += part[channels * a:channels * (a + 1), width:]

    kgs = []
    for h, y in enumerate((0, rows - 1)):
        g = [cot[c, y:y + 1, :] for c in range(3)]
        terms = frame_terms(taps, k[:, width * h:width * (h + 1)], g, bands)
        for f, (_, _, w) in enumerate(terms):
            for c in range(3):
                gf[3 * f + c, y:y + 32] += w[32 * c:32 * c + 32]
        kgs.append(tap_grads(y, [t[:2] for t in terms]))
    accumulate(0, rows - 1, edges, *kgs)

    def step(m, carry):
        ya = 2 * m + 1
        pair = jnp.concatenate(
            [fb[pl.ds(ya + h - 1, 3)].reshape(9 * channels, width) for h in range(2)], 1)
        kga, kgb = [
            tap_grads(ya + h, [(bst[ya + h - 1, f], ust[ya + h - 1, f]) for f in range(2)])
            for h in range(2)]
        accumulate(ya, ya + 1, pair, kga, kgb)
        return carry

    lax.fori_loop(0, rows // 2 - 1, step, 0, unroll=UNROLL_LATE)

    for y in range(rows):
        gfeat[pl.ds(y, channels, stride=rows), :] = acc[y + 1]
    rim_up[:channels] = acc[0].astype(BF16)
    rim_dn[:channels] = acc[rows + 1].astype(BF16)
    for n in range(6):
        gf[n] = pltpu.roll(gf[n], width - rim - 64 * (n // 3), 1)
        gframe[n] = gf[n, rim:rim + rows]
        at = channels + n * rim
        rim_up[at:at + rim] = gf[n, :rim].astype(BF16)
        rim_dn[at:at + rim] = gf[n, rim + rows:rim + rows + rim].astype(BF16)
    pack(wg[...], flat)
    count, size = parts_ref.shape[:2]
    for n in range(count):
        parts_ref[n] = flat[size * n:size * (n + 1)]


def pack(value, flat):
    full = value.shape[1] // 128
    for n in range(full):
        flat[128 * n:128 * (n + 1)] = value[:, 128 * n:128 * (n + 1)]
    tail = value[:, 128 * full:]
    flat[128 * full:] = jnp.concatenate([tail[:64], tail[64:]], 1)


def unpack_kernel(taps, factor, parts_ref, out, flat):
    count, size = parts_ref.shape[:2]
    for n in range(count):
        flat[size * n:size * (n + 1)] = parts_ref[n].astype(F32)
    full = out.shape[1] // 128
    tail = flat[128 * full:]
    blocks = [flat[128 * n:128 * (n + 1)] for n in range(full)]
    blocks.append(jnp.concatenate([tail[:, :64], tail[:, 64:]], 0))
    value = jnp.concatenate(blocks, 1) * factor
    for n, group in enumerate((1, 0, 3, 2)):
        out[taps * n:taps * (n + 1)] = value[32 * group:32 * group + taps]


def order(hw, taps):
    hw = hw.reshape(2, 2, taps, -1)[:, ::-1]
    return jnp.pad(hw, ((0, 0), (0, 0), (0, 32 - taps), (0, 0))).reshape(128, -1)


def vmem_call(kernel, outs, scratch, *operands):
    vm = pl.BlockSpec(memory_space=pltpu.VMEM)
    return pl.pallas_call(
        kernel,
        out_shape=[jax.ShapeDtypeStruct(*o) for o in outs],
        in_specs=[vm] * len(operands),
        out_specs=[vm] * len(outs),
        scratch_shapes=[pltpu.VMEM(*o) for o in scratch],
        compiler_params=pltpu.CompilerParams(vmem_limit_bytes=VMEM_GRANT),
    )(*operands)


def early(feat, cot, wfwd, taps):
    channels, rows, width = feat.shape
    return vmem_call(
        functools.partial(early_kernel, taps),
        [((rows, 3 * channels, width), BF16), ((rows - 2, 2, width, 2 * width), BF16),
         ((rows - 2, 2, 192, width), BF16), ((6, rows + 32, width), F32)],
        [((channels * rows, width), F32)],
        feat, cot, wfwd)


def late(halo_up, halo_dn, frames, cot, wfwd, wbwd, held, taps, parts):
    rows, width = held[0].shape[0], held[0].shape[2]
    channels = held[0].shape[1] // 3
    columns = 9 * channels
    rim_shape = (halo_up.shape, BF16)
    return vmem_call(
        functools.partial(late_kernel, taps),
        [((parts, columns // parts, 128), F32), ((channels * rows, width), F32),
         ((6, rows, width), F32), rim_shape, rim_shape],
        [((6, rows + 32, width), F32), ((6, rows + 32, width), F32),
         ((rows + 2, channels, width), F32), ((128, columns), F32), ((columns, 128), F32)],
        halo_up, halo_dn, frames, cot, wfwd, wbwd, *held)


def both_weights(hw, taps, channels):
    wfwd = order(hw, taps)
    wbwd = wfwd.reshape(128, 3, 3, channels).transpose(1, 3, 2, 0).reshape(3 * channels, 3 * 128)
    return wfwd, wbwd


def fan_kernel(parts_ref, out):
    total = jnp.sum(parts_ref[...], 0).astype(out.dtype)
    for n in range(out.shape[0]):
        out[n] = total


def fan(parts, count, dtype):
    return vmem_call(fan_kernel, [((count,) + parts.shape[1:], dtype)], [], parts)[0]


def unpack(parts, taps, factor):
    count, size, _ = parts.shape
    return vmem_call(
        functools.partial(unpack_kernel, taps, factor),
        [((4 * taps, count * size), F32)], [((count * size, 128), F32)], parts)[0]


PLANE, LINE, TILE = ("y", "core", "x"), ("zl", "zh"), ("x", "zh")


def step(frames, features, cotangent, head_weight):
    taps = head_weight.shape[0] // 4
    rim = (taps - 1) // 2
    feat, frame, cot = features[0], frames[0], cotangent[0]
    channels, rows, width = feat.shape
    tiles, plane, line = lax.axis_size(TILE), lax.axis_size(PLANE), lax.axis_size(LINE)
    down = [(i, i + 1) for i in range(tiles - 1)]
    up = [(i + 1, i) for i in range(tiles - 1)]

    def halo(row, part):
        return jnp.concatenate([feat[:, row], part.reshape(6 * rim, width)], 0)

    halo_up = lax.ppermute(halo(rows - 1, frame[:, :, rows - rim:]), TILE, down)
    halo_dn = lax.ppermute(halo(0, frame[:, :, :rim]), TILE, up)
    wfwd, wbwd = both_weights(head_weight, taps, channels)
    held = early(feat, cot, wfwd, taps)
    parts, gfeat, gframe, rim_up, rim_dn = late(
        halo_up, halo_dn, frame, cot, wfwd, wbwd, held, taps, plane)

    from_up = lax.ppermute(rim_dn, TILE, down)
    from_dn = lax.ppermute(rim_up, TILE, up)

    terms = lax.all_to_all(parts, PLANE, 0, 0)
    terms = lax.all_to_all(fan(terms, line, F32), LINE, 0, 0)
    total = lax.all_to_all(fan(terms, plane, BF16), PLANE, 0, 0)
    from_up, from_dn = from_up.astype(F32), from_dn.astype(F32)
    pixels = plane * line * rows * width
    grad_weight = unpack(total, taps, pixels ** -0.5)

    gfeat = gfeat.reshape(channels, rows, width)
    gfeat = (gfeat + jnp.pad(from_up[:channels, None], ((0, 0), (0, rows - 1), (0, 0)))
             + jnp.pad(from_dn[:channels, None], ((0, 0), (rows - 1, 0), (0, 0))))
    gframe = (gframe
              + jnp.pad(from_up[channels:].reshape(6, rim, width), ((0, 0), (0, rows - rim), (0, 0)))
              + jnp.pad(from_dn[channels:].reshape(6, rim, width), ((0, 0), (rows - rim, 0), (0, 0))))
    return grad_weight, gfeat[None], gframe.reshape(1, 2, 3, rows, width)


def solution(mesh):
    fine = Mesh(mesh.devices.reshape(8, 4, 2, 4, 2), ("zl", "y", "core", "x", "zh"))
    pairs, tile = ("zl", "y", "core"), ("x", "zh")
    in_specs = (
        P(pairs, None, None, tile, None),
        P(pairs, None, tile, None),
        P(pairs, None, tile, None),
        P(),
    )
    out_specs = (P(), P(pairs, None, tile, None), P(pairs, None, None, tile, None))
    return jax.shard_map(step, mesh=fine, in_specs=in_specs, out_specs=out_specs, check_vma=False)
```

time: 124 us -> 107 us (0.86)
  blocking collectives: 21.2 us -> 0 us
  starting transfers between devices: 40.6 us -> 54.1 us
  Pallas kernels: 21.3 us -> 13.8 us
  local copies, waits for them, and re-layouts: 7.54 us -> 4.56 us
  waiting for transfers between devices: 30.7 us -> 32.5 us
    all_to_all x2 -> x3, starting transfers between devices: 9.75 us -> 31.7 us  [the longest x1 13.7 us: step(): total = lax.all_to_all(fan(terms, plane, BF16), PLANE, 0, 0)]
    all_to_all x1 -> x0, blocking collectives: 21.2 us -> none  [shards(): own = jnp.sum(lax.all_to_all(parts, PLANE, 0, 0), 0)]
    all_to_all x2 -> x3, waiting for transfers between devices: 8.16 us -> 26 us  [the longest x1 13.2 us: step(): terms = lax.all_to_all(fan(terms, line, F32), LINE, 0, 0)]
    ppermute x4, waiting for transfers between devices: 22.5 us -> 6.45 us  [the longest x1 6.45 us: step(): halo_dn = lax.ppermute(halo(0, frame[:, :, :rim]), TILE, up)]
    ppermute x4, starting transfers between devices: 30.8 us -> 22.4 us  [the longest x1 16.3 us: step(): halo_up = lax.ppermute(halo(rows - 1, frame[:, :, rows - rim:]), TILE, down)]
    pallas_call x2 -> x5, Pallas kernels: 21.3 us -> 13.8 us  [vmem_call(): pl.pallas_call(kernel, out_shape=[jax.ShapeDtypeStruct(*o) for o in outs]...]
    unnamed x21 -> x9, local copies, waits for them, and re-layouts: 4.6 us -> 2.17 us
    broadcast_in_dim x4 -> x2, local copies, waits for them, and re-layouts: 1.47 us -> 0.01 us  [the longest x1 0.01 us: step(): from_up[:channels, None]]
  transfers between devices with their start and end apart: 6 -> 7, of which waited for: 3 -> 4; matrix products, arithmetic and copies ran while one was open for 3% -> 3% of each run, Pallas kernels for 0% -> 5%
where the time goes in v2:
time: 107 us
  starting transfers between devices  54.1 us (51%)
  waiting for transfers between devices  32.5 us (30%)
  Pallas kernels  13.8 us (13%)
  local copies, waits for them, and re-layouts  4.56 us (4%)
    ppermute x1, starting transfers between devices, step(): halo_up = lax.ppermute(halo(rows - 1, frame[:, :, rows - rim:]), TILE, down)  16.3 us
    pallas_call x5, Pallas kernels, vmem_call(): pl.pallas_call(kernel, out_shape=[jax.ShapeDtypeStruct(*o) for o in outs]...  13.8 us
    all_to_all x1, starting transfers between devices, step(): total = lax.all_to_all(fan(terms, plane, BF16), PLANE, 0, 0)  13.7 us
    all_to_all x1, waiting for transfers between devices, step(): terms = lax.all_to_all(fan(terms, line, F32), LINE, 0, 0)  13.2 us
    all_to_all x1, starting transfers between devices, step(): terms = lax.all_to_all(parts, PLANE, 0, 0)  11.1 us
    all_to_all x1, waiting for transfers between devices, step(): total = lax.all_to_all(fan(terms, plane, BF16), PLANE, 0, 0)  7.61 us
    all_to_all x1, starting transfers between devices, step(): terms = lax.all_to_all(fan(terms, line, F32), LINE, 0, 0)  6.91 us
    ppermute x1, waiting for transfers between devices, step(): halo_dn = lax.ppermute(halo(0, frame[:, :, :rim]), TILE, up)  6.45 us
  transfers between devices with their start and end apart: 7, of which 4 were waited for; matrix products, arithmetic and copies ran while one was open for 3% of the time, Pallas kernels for 5%

profile of v2, /device:TPU:1, one launch (start us, length us, event | category | flops | bytes accessed | tf_op | source)
XLA Modules:
  0.0 106.7 jit_solution(16359283745248729973)
XLA Ops:
  0.6 0.0 copy-start
  0.6 0.0 copy-start.2
  0.7 0.8 fusion.2
  1.5 0.0 copy-start.1
  1.5 1.0 copy.24
  2.6 16.3 %collective-permute-start = (bf16[142,128]{1,0:T(8,128)(2,1)S(1)}, bf16[142,128]{1,0:T(8,128)(2,1)S(1)}, u32[]{:S(2)}, u32[]{:S(2)}) collective-permute-start(bf16[142,128]{1,0:T(8,128)(2,1)S(1)} %pad_maximum_fusion), channel_id=1, source_target_pairs={{0,1},{1,2},{2,3},{3,4},{4,5},{5,6},{6,7},{8,9},{9,10},{10,11},{11... | collective-permute-start | bytes 109064 | tf_op jit(solution)/shard_map/ppermute | solution.py:288
  18.9 1.3 %collective-permute-start.1 = (bf16[142,128]{1,0:T(8,128)(2,1)S(1)}, bf16[142,128]{1,0:T(8,128)(2,1)S(1)}, u32[]{:S(2)}, u32[]{:S(2)}) collective-permute-start(bf16[142,128]{1,0:T(8,128)(2,1)S(1)} %pad_maximum_fusion.1), channel_id=1, source_target_pairs={{1,0},{2,1},{3,2},{4,3},{5,4},{6,5},{7,6},{9,8},{10,9},{11,10},{12... | collective-permute-start | bytes 109064 | tf_op jit(solution)/shard_map/ppermute | solution.py:289
  20.2 1.0 reshape.35
  21.2 0.2 reshape_reshape.3
  21.4 0.3 copy.11
  21.7 0.0 copy-done
  21.7 0.0 copy-done.2
  21.8 4.1 %shard_map.67 = (bf16[16,192,128]{2,1,0:T(8,128)(2,1)S(1)}, bf16[14,2,128,256]{3,2,1,0:T(8,128)(2,1)S(1)}, bf16[14,2,192,128]{3,2,1,0:T(8,128)(2,1)S(1)}, f32[6,48,128]{2,1,0:T(8,128)S(1)}) custom-call(bf16[64,16,128]{2,1,0:T(8,128)(2,1)S(1)} %bitcast.29, f32[3,16,128]{2,1,0:T(8,128)S(1)} %bitcast.34, bf16[128,576]{1,0:T(8,128)(2,1)S(1)} %bitcast.27), custom_call_target="tpu_custom_call" | custom-call | tf_op jit(solution)/shard_map/pallas_call | solution.py:216
  25.8 0.0 collective-permute-done.halo_up
  25.9 6.4 %collective-permute-done.1.halo_dn = bf16[142,128]{1,0:T(8,128)(2,1)S(1)} collective-permute-done((bf16[142,128]{1,0:T(8,128)(2,1)S(1)}, bf16[142,128]{1,0:T(8,128)(2,1)S(1)}, u32[]{:S(2)}, u32[]{:S(2)}) %collective-permute-start.1) | collective-permute-done | bytes 36384 | tf_op jit(solution)/shard_map/ppermute | solution.py:289
  32.3 7.4 %shard_map.68 = (f32[32,18,128]{2,1,0:T(8,128)}, f32[1024,128]{1,0:T(8,128)S(1)}, f32[6,16,128]{2,1,0:T(8,128)S(1)}, bf16[142,128]{1,0:T(8,128)(2,1)S(1)}, bf16[142,128]{1,0:T(8,128)(2,1)S(1)}) custom-call(bf16[142,128]{1,0:T(8,128)(2,1)S(1)} %collective-permute-done.halo_up, bf16[142,128]{1,0:T(8,128)(2,1)S(1)} %collective-permute-done.1.halo_dn, ...), custom_call_target="tpu_custom_call" | custom-call | tf_op jit(solution)/shard_map/pallas_call | solution.py:216
  39.7 11.1 %all-to-all-start = ((f32[32,18,128]{2,1,0:T(8,128)}), f32[32,18,128]{2,1,0:T(8,128)S(1)}, u32[]{:S(2)}, u32[]{:S(2)}) async-start(f32[32,18,128]{2,1,0:T(8,128)} %get-tuple-element.16), calls=%async_computation | async-start | bytes 786432 | tf_op jit(solution)/shard_map/all_to_all | solution.py:298
  50.8 3.5 %collective-permute-start.2 = (bf16[142,128]{1,0:T(8,128)(2,1)S(1)}, bf16[142,128]{1,0:T(8,128)(2,1)S(1)}, u32[]{:S(2)}, u32[]{:S(2)}) collective-permute-start(bf16[142,128]{1,0:T(8,128)(2,1)S(1)} %get-tuple-element.18), channel_id=1, source_target_pairs={{0,1},{1,2},{2,3},{3,4},{4,5},{5,6},{6,7},{8,9},{9,10},{10,11},{11... | collective-permute-start | bytes 109064 | tf_op jit(solution)/shard_map/ppermute | solution.py:295
  54.4 1.3 %collective-permute-start.3 = (bf16[142,128]{1,0:T(8,128)(2,1)S(1)}, bf16[142,128]{1,0:T(8,128)(2,1)S(1)}, u32[]{:S(2)}, u32[]{:S(2)}) collective-permute-start(bf16[142,128]{1,0:T(8,128)(2,1)S(1)} %get-tuple-element.19), channel_id=1, source_target_pairs={{1,0},{2,1},{3,2},{4,3},{5,4},{6,5},{7,6},{9,8},{10,9},{11,10},{12... | collective-permute-start | bytes 109064 | tf_op jit(solution)/shard_map/ppermute | solution.py:296
  55.7 0.0 collective-permute-done.2
  55.7 5.3 %all-to-all-done.parts_ref = f32[32,18,128]{2,1,0:T(8,128)S(1)} async-done(((f32[32,18,128]{2,1,0:T(8,128)}), f32[32,18,128]{2,1,0:T(8,128)S(1)}, u32[]{:S(2)}, u32[]{:S(2)}) %all-to-all-start) | async-done | bytes 294944 | tf_op jit(solution)/shard_map/all_to_all | solution.py:298
  61.0 0.7 shard_map.69
  61.7 6.9 %all-to-all-start.1 = ((f32[16,18,128]{2,1,0:T(8,128)}), f32[16,18,128]{2,1,0:T(8,128)S(1)}, u32[]{:S(2)}, u32[]{:S(2)}) async-start(f32[16,18,128]{2,1,0:T(8,128)} %shard_map.69), calls=%async_computation.1 | async-start | bytes 393216 | tf_op jit(solution)/shard_map/all_to_all | solution.py:299
  68.7 0.0 collective-permute-done.3
  68.7 0.2 fusion.1
  68.9 1.1 %copy.14 = f32[1,64,16,128]{3,2,1,0:T(8,128)} copy(f32[1,64,16,128]{3,1,2,0:T(8,128)S(1)} %fusion.1) | data formatting | bytes 1048576
  70.0 13.2 %all-to-all-done.1.parts_ref = f32[16,18,128]{2,1,0:T(8,128)S(1)} async-done(((f32[16,18,128]{2,1,0:T(8,128)}), f32[16,18,128]{2,1,0:T(8,128)S(1)}, u32[]{:S(2)}, u32[]{:S(2)}) %all-to-all-start.1) | async-done | bytes 147488 | tf_op jit(solution)/shard_map/all_to_all | solution.py:299
  83.2 0.7 shard_map.70
  83.9 13.7 %all-to-all-start.2 = ((bf16[32,18,128]{2,1,0:T(8,128)(2,1)}), bf16[32,18,128]{2,1,0:T(8,128)(2,1)S(1)}, u32[]{:S(2)}, u32[]{:S(2)}) async-start(bf16[32,18,128]{2,1,0:T(8,128)(2,1)} %shard_map.70), calls=%async_computation.2 | async-start | bytes 393216 | tf_op jit(solution)/shard_map/all_to_all | solution.py:300
  97.6 0.6 pad_add_fusion
  98.3 7.6 %all-to-all-done.2.parts_ref = bf16[32,18,128]{2,1,0:T(8,128)(2,1)S(1)} async-done(((bf16[32,18,128]{2,1,0:T(8,128)(2,1)}), bf16[32,18,128]{2,1,0:T(8,128)(2,1)S(1)}, u32[]{:S(2)}, u32[]{:S(2)}) %all-to-all-start.2) | async-done | bytes 147488 | tf_op jit(solution)/shard_map/all_to_all | solution.py:300
  105.9 0.8 shard_map.71
  (17 shorter events, 0.2 us)
Async XLA Ops:
  0.6 21.1 %copy-start = (bf16[1,64,16,128]{3,2,1,0:T(8,128)(2,1)S(1)}, bf16[1,64,16,128]{3,2,1,0:T(8,128)(2,1)}, u32[]{:S(2)}) copy-start(bf16[1,64,16,128]{3,2,1,0:T(8,128)(2,1)} %param.5) | copy-start | bytes 786436
  0.6 21.1 %copy-start.2 = (f32[1,3,16,128]{3,2,1,0:T(8,128)S(1)}, f32[1,3,16,128]{3,2,1,0:T(8,128)}, u32[]{:S(2)}) copy-start(f32[1,3,16,128]{3,2,1,0:T(8,128)} %param.6) | copy-start | bytes 73732
  1.5 30.8 %copy-start.1 = (bf16[1,2,3,16,128]{4,3,2,1,0:T(8,128)(2,1)S(1)}, bf16[1,2,3,16,128]{4,3,2,1,0:T(8,128)(2,1)}, u32[]{:S(2)}) copy-start(bf16[1,2,3,16,128]{4,3,2,1,0:T(8,128)(2,1)} %param.4) | copy-start | bytes 73732
  2.6 23.3 %collective-permute-start = (bf16[142,128]{1,0:T(8,128)(2,1)S(1)}, bf16[142,128]{1,0:T(8,128)(2,1)S(1)}, u32[]{:S(2)}, u32[]{:S(2)}) collective-permute-start(bf16[142,128]{1,0:T(8,128)(2,1)S(1)} %pad_maximum_fusion), channel_id=1, source_target_pairs={{0,1},{1,2},{2,3},{3,4},{4,5},{5,6},{6,7},{8,9},{9,10},{10,11},{11... | collective-permute-start | bytes 109064 | tf_op jit(solution)/shard_map/ppermute | solution.py:288
  18.9 13.4 %collective-permute-start.1 = (bf16[142,128]{1,0:T(8,128)(2,1)S(1)}, bf16[142,128]{1,0:T(8,128)(2,1)S(1)}, u32[]{:S(2)}, u32[]{:S(2)}) collective-permute-start(bf16[142,128]{1,0:T(8,128)(2,1)S(1)} %pad_maximum_fusion.1), channel_id=1, source_target_pairs={{1,0},{2,1},{3,2},{4,3},{5,4},{6,5},{7,6},{9,8},{10,9},{11,10},{12... | collective-permute-start | bytes 109064 | tf_op jit(solution)/shard_map/ppermute | solution.py:289
  39.7 21.2 %all-to-all-start = ((f32[32,18,128]{2,1,0:T(8,128)}), f32[32,18,128]{2,1,0:T(8,128)S(1)}, u32[]{:S(2)}, u32[]{:S(2)}) async-start(f32[32,18,128]{2,1,0:T(8,128)} %get-tuple-element.16), calls=%async_computation | async-start | bytes 786432 | tf_op jit(solution)/shard_map/all_to_all | solution.py:298
  50.8 4.9 %collective-permute-start.2 = (bf16[142,128]{1,0:T(8,128)(2,1)S(1)}, bf16[142,128]{1,0:T(8,128)(2,1)S(1)}, u32[]{:S(2)}, u32[]{:S(2)}) collective-permute-start(bf16[142,128]{1,0:T(8,128)(2,1)S(1)} %get-tuple-element.18), channel_id=1, source_target_pairs={{0,1},{1,2},{2,3},{3,4},{4,5},{5,6},{6,7},{8,9},{9,10},{10,11},{11... | collective-permute-start | bytes 109064 | tf_op jit(solution)/shard_map/ppermute | solution.py:295
  54.4 14.3 %collective-permute-start.3 = (bf16[142,128]{1,0:T(8,128)(2,1)S(1)}, bf16[142,128]{1,0:T(8,128)(2,1)S(1)}, u32[]{:S(2)}, u32[]{:S(2)}) collective-permute-start(bf16[142,128]{1,0:T(8,128)(2,1)S(1)} %get-tuple-element.19), channel_id=1, source_target_pairs={{1,0},{2,1},{3,2},{4,3},{5,4},{6,5},{7,6},{9,8},{10,9},{11,10},{12... | collective-permute-start | bytes 109064 | tf_op jit(solution)/shard_map/ppermute | solution.py:296
  61.7 21.5 %all-to-all-start.1 = ((f32[16,18,128]{2,1,0:T(8,128)}), f32[16,18,128]{2,1,0:T(8,128)S(1)}, u32[]{:S(2)}, u32[]{:S(2)}) async-start(f32[16,18,128]{2,1,0:T(8,128)} %shard_map.69), calls=%async_computation.1 | async-start | bytes 393216 | tf_op jit(solution)/shard_map/all_to_all | solution.py:299
  83.9 22.0 %all-to-all-start.2 = ((bf16[32,18,128]{2,1,0:T(8,128)(2,1)}), bf16[32,18,128]{2,1,0:T(8,128)(2,1)S(1)}, u32[]{:S(2)}, u32[]{:S(2)}) async-start(bf16[32,18,128]{2,1,0:T(8,128)(2,1)} %shard_map.70), calls=%async_computation.2 | async-start | bytes 393216 | tf_op jit(solution)/shard_map/all_to_all | solution.py:300
